TPU v7x, 32 devices: a whole 2x2x4 slice. The times are simulated.
32 devices in a mesh: det: 8 (over y, x, core), row: 4 (over z).
Axes of the slice: x: 2, y: 2, z: 4, core: 2. Of those that a mesh axis runs over, the one named last changes fastest.
Arguments:
- coefficients: bfloat16 [8, 2048, 200], P('det', 'row'), may hold values from -1 to 1
- amplitudes: bfloat16 [8], P('det'), may hold values from -3 to 3
- plan: int32 [8, 2, 1], P('det'), may hold values 0 or 1
Outputs:
- density: float32 [2048, 2048], P('det', 'row')
All inputs are finite; a program needn't handle non-finite values. No bound on the sum of `plan` on one device may be relied on, other than what follows from the above.
Results may differ from a plain program's by a relative error of at most 0.0024.
Values may be sent and summed in bfloat16 or wider, within the bound.
A program may use at most 64 MiB of HBM per device.

v0:
```python
import functools

import jax
import jax.numpy as jnp
from jax import lax
from jax.experimental import pallas as pl
from jax.experimental.pallas import tpu as pltpu
from jax.sharding import PartitionSpec as P

ORDER = 2
F32 = jnp.float32
BF16 = jnp.bfloat16


def each(count, body):
    if count <= 8:
        for i in range(count):
            body(i)
    else:
        lax.fori_loop(0, count, lambda i, c: (body(i), c)[1], 0)


def inverse_of(correlation):
    size = correlation.shape[0]
    row = lax.broadcasted_iota(jnp.int32, (size, size), 0)
    col = lax.broadcasted_iota(jnp.int32, (size, size), 1)
    identity = jnp.where(row == col, 1.0, 0.0).astype(F32)
    remainder = identity - correlation
    inverse = identity + remainder
    for level in range(ORDER - 1):
        inverse = identity + jnp.dot(
            remainder, inverse, precision=lax.Precision.HIGHEST, preferred_element_type=F32
        )
    return inverse


def gram(a, b):
    return lax.dot_general(a, b, (((0,), (0,)), ((), ())), preferred_element_type=F32)


def against(a, b):
    return lax.dot_general(a, b, (((1,), (1,)), ((), ())), preferred_element_type=F32)


def parts_of(size, count):
    step = -(-size // (8 * count)) * 8
    return [(start, min(step, size - start)) for start in range(0, size, step)]


def kernel(
    n, ring, c_ref, amp_ref, plan_ref, out_ref,
    cw, vis, amps, own, sum_in, sum_out, s0, pieces, folded, wide,
    local_sem, cw_send, cw_recv, sum_send, sum_recv, vis_send, vis_recv,
    piece_send, piece_recv, chip_send, pair_send, folded_recv,
):
    det = lax.axis_index("det")
    row = lax.axis_index("row")
    rows = out_ref.shape[0]
    width = pieces.shape[2]
    per_block = n // ring
    chips = n // 2
    chip, core = det // 2, lax.rem(det, 2)
    partner = chip * 2 + (1 - core)
    has_right, has_left = row < ring - 1, row > 0
    toward = (has_right, has_left)
    chunks = parts_of(own.shape[0], 4)

    def remote(src, dst, send, recv, **where):
        return pltpu.make_async_remote_copy(
            src_ref=src, dst_ref=dst, send_sem=send, recv_sem=recv,
            device_id=where, device_id_type=pl.DeviceIdType.MESH,
        )

    keep = pltpu.make_async_copy(c_ref, cw.at[row], local_sem)
    keep.start()

    barrier = pltpu.get_barrier_semaphore()

    def greet(i):
        peer = lax.rem(det + 1 + i, n)
        pl.semaphore_signal(barrier, inc=1, device_id={"det": peer}, device_id_type=pl.DeviceIdType.MESH)

    each(n - 1, greet)

    for side in (0, 1):

        @pl.when(toward[side])
        def _():
            peer = row + 1 - 2 * side
            pl.semaphore_signal(barrier, inc=1, device_id={"row": peer}, device_id_type=pl.DeviceIdType.MESH)

    amps[0] = jnp.broadcast_to(amp_ref[...].astype(F32), amps.shape[1:])
    pl.semaphore_wait(barrier, n - 1 + has_right.astype(jnp.int32) + has_left.astype(jnp.int32))

    halves = parts_of(own.shape[0], 2)

    def along(block, side, half):
        span = cw.at[block, pl.ds(*halves[half])]
        return remote(
            span, span, cw_send.at[block, side, half], cw_recv.at[block, half], row=row + 1 - 2 * side
        )

    def pass_on(block, side, half, wait=False):
        @pl.when(toward[side])
        def _():
            copy = along(block, side, half)
            if wait:
                copy.wait_send()
            else:
                copy.start()

    def chunk_copy(k, side):
        span = pl.ds(*chunks[k])
        return remote(
            sum_out.at[side, span], sum_in.at[side, span], sum_send.at[side, k], sum_recv.at[side, k],
            row=row + 1 - 2 * side,
        )

    def sums(side, first):
        for k, (start, length) in enumerate(chunks):
            span = pl.ds(start, length)
            if first:
                sum_in[side, span] = jnp.zeros((length, own.shape[1]), F32)
                sum_out[side, span] = own[span]
            else:
                chunk_copy(k, side).wait_recv()
                sum_out[side, span] = own[span] + sum_in[side, span]

            @pl.when(toward[side])
            def _():
                chunk_copy(k, side).start()

    def piece(block, k):
        target = block * per_block + k
        start = pl.multiple_of(k * rows // width * width, width)
        return target, remote(
            cw.at[block, :, pl.ds(start, width)], pieces.at[det],
            piece_send.at[block, k], piece_recv.at[det], det=target,
        )

    def hand_out(block, wait=False):
        def one(k):
            target, copy = piece(block, k)

            @pl.when(target != det)
            def _():
                if wait:
                    copy.wait_send()
                else:
                    copy.start()

        each(per_block, one)

    following = lax.rem(det + 1, n)
    visit = remote(c_ref, vis, vis_send.at[0], vis_recv.at[0], det=following)
    visit_amp = remote(amps.at[0], amps.at[1], vis_send.at[1], vis_recv.at[1], det=following)
    visit.start()
    visit_amp.start()
    keep.wait()
    for half in (0, 1):
        for side in (0, 1):
            pass_on(row, side, half)
    s0[...] = against(c_ref[...], c_ref[...])
    visit.wait_recv()
    own[...] = against(vis[...], c_ref[...])

    @pl.when(row == 0)
    def _():
        sums(0, True)

    @pl.when(row == ring - 1)
    def _():
        sums(1, True)

    hand_out(row)

    def arrive(distance):
        for side in (0, 1):
            block = row - distance if side == 0 else row + distance

            @pl.when((block >= 0) & (block < ring))
            def _():
                along(block, side, 0).wait_recv()
                pass_on(block, side, 0)

        for side in (0, 1):
            block = row - distance if side == 0 else row + distance

            @pl.when((block >= 0) & (block < ring))
            def _():
                along(block, side, 1).wait_recv()
                pass_on(block, side, 1)
                hand_out(block)
                s0[...] += against(cw[block], cw[block])

    def gather_sums(distance):
        @pl.when(row == distance)
        def _():
            sums(0, False)

        @pl.when(row == ring - 1 - distance)
        def _():
            sums(1, False)

    for distance in range(1, ring - 1):
        arrive(distance)
        gather_sums(distance)
    arrive(ring - 1)
    visit_amp.wait_recv()
    amp = amps[0, 0:1, 0:1]
    masks = plan_ref[...].astype(F32)
    weight = amp * amp * masks[0:1, 0:1]
    scaled = (weight * inverse_of(s0[...])).astype(BF16)
    total = jnp.dot(scaled, c_ref[...], preferred_element_type=F32)
    gather_sums(ring - 1)
    weight = amps[1, 0:1, 0:1] * amp * masks[1:2, 0:1]
    correlation = own[...] + sum_in[0] + sum_in[1]
    scaled = (weight * inverse_of(correlation)).astype(BF16)
    total = total + jnp.dot(scaled, vis[...], preferred_element_type=F32)
    folded[det] = total.astype(BF16)

    def to_chip(i):
        target = lax.rem(chip + 1 + i, chips) * 2 + core
        return remote(folded.at[det], folded.at[det], chip_send.at[i], folded_recv.at[det], det=target)

    def to_pair(source):
        return remote(
            folded.at[source], folded.at[source], pair_send.at[source], folded_recv.at[source], det=partner
        )

    each(chips - 1, lambda i: to_chip(i).start())
    to_pair(det).start()

    def landed(source):
        to_pair(source).wait_recv()

    sink = out_ref if width == rows else wide

    def add(source):
        remote(
            cw.at[0, :, pl.ds(0, width)], pieces.at[source], piece_send.at[0, 0], piece_recv.at[source],
            det=partner,
        ).wait_recv()
        sink[...] += gram(pieces[source], folded[source])

    own_start = lax.rem(det, per_block) * rows // width * width
    mine = cw[det // per_block, :, pl.ds(pl.multiple_of(own_start, width), width)]
    sink[...] = gram(mine, folded[det])
    landed(partner)
    add(partner)

    def relay(i):
        other = lax.rem(chip + chips - 1 - i, chips) * 2
        landed(other + core)
        to_pair(other + core).start()
        add(other + core)

    def relayed(i):
        other = lax.rem(chip + chips - 1 - i, chips) * 2
        landed(other + 1 - core)
        add(other + 1 - core)

    each(chips - 1, relay)
    each(chips - 1, relayed)
    if width != rows:
        out_ref[...] = wide[pl.ds(pl.multiple_of(lax.rem(det * rows, width), rows), rows)]

    visit.wait_send()
    visit_amp.wait_send()
    for side in (0, 1):
        for half in (0, 1):
            pass_on(row, side, half, wait=True)

        @pl.when(toward[side])
        def _():
            for k in range(len(chunks)):
                chunk_copy(k, side).wait_send()

    hand_out(row, wait=True)
    for distance in range(1, ring):
        for side in (0, 1):
            block = row - distance if side == 0 else row + distance

            @pl.when((block >= 0) & (block < ring))
            def _():
                for half in (0, 1):
                    pass_on(block, side, half, wait=True)
                hand_out(block, wait=True)

    each(chips - 1, lambda i: to_chip(i).wait_send())
    to_pair(det).wait_send()
    each(chips - 1, lambda i: to_pair(lax.rem(chip + chips - 1 - i, chips) * 2 + core).wait_send())


def on_device(coefficients, amplitudes, plan):
    n, ring = lax.axis_size("det"), lax.axis_size("row")
    if coefficients.shape[0] != 1 or plan.shape[1] != 2:
        raise ValueError("unsupported sizes")
    block = jnp.swapaxes(coefficients, 1, 2)[0]
    orbitals, size = block.shape
    rows = size * ring // n
    width = max(rows, 128)
    dma = pltpu.SemaphoreType.DMA
    return pl.pallas_call(
        functools.partial(kernel, n, ring),
        out_shape=jax.ShapeDtypeStruct((rows, size), F32),
        in_specs=[pl.BlockSpec(memory_space=pltpu.VMEM)] * 3,
        out_specs=pl.BlockSpec(memory_space=pltpu.VMEM),
        scratch_shapes=[
            pltpu.VMEM((ring, orbitals, size), BF16),
            pltpu.VMEM((orbitals, size), BF16),
            pltpu.VMEM((2, 8, 128), F32),
            pltpu.VMEM((orbitals, orbitals), F32),
            pltpu.VMEM((2, orbitals, orbitals), F32),
            pltpu.VMEM((2, orbitals, orbitals), F32),
            pltpu.VMEM((orbitals, orbitals), F32),
            pltpu.VMEM((n, orbitals, width), BF16),
            pltpu.VMEM((n, orbitals, size), BF16),
            pltpu.VMEM((width, size) if width != rows else (8, 128), F32),
            dma, dma((ring, 2, 2)), dma((ring, 2)), dma((2, 4)), dma((2, 4)), dma((2,)), dma((2,)),
            dma((ring, n // ring)), dma((n,)), dma((n // 2,)), dma((n,)), dma((n,)),
        ],
        compiler_params=pltpu.CompilerParams(
            collective_id=0, has_side_effects=True, vmem_limit_bytes=60 * 1024 * 1024
        ),
    )(block, amplitudes.reshape(1, 1), plan.reshape(2, 1))


def solution(mesh):
    placed = (P("det", "row", None), P("det"), P("det", None, None))
    return jax.shard_map(
        on_device, mesh=mesh, in_specs=placed, out_specs=P("det", "row"), check_vma=False
    )
```

profile of v0, /device:TPU:7, one launch (start us, length us, event | category | flops | bytes accessed | tf_op | source)
XLA Modules:
  0.0 44.6 jit_solution(2494897733333441492)
XLA Ops:
  0.7 0.0 copy-start
  0.7 0.6 %copy-done = s32[1,2,1]{1,2,0:T(1,128)S(1)} copy-done((s32[1,2,1]{1,2,0:T(1,128)S(1)}, s32[1,2,1]{1,2,0:T(1,128)}, u32[]{:S(2)}) %copy-start) | copy-done | bytes 32
  1.3 0.6 %copy.4.plan_ref = s32[2,1]{1,0:T(2,128)} copy(s32[2,1]{0,1:T(1,128)S(1)} %bitcast.7) | data formatting | bytes 16 | tf_op jit(solution)/shard_map/reshape | solution.py:326
  2.0 40.8 %shard_map.37 = f32[256,512]{1,0:T(8,128)} custom-call(bf16[200,512]{1,0:T(8,128)(2,1)} %bitcast.6, bf16[1,1]{1,0:T(2,128)(2,1)} %bitcast.5.amp_ref, s32[2,1]{1,0:T(2,128)} %copy.4.plan_ref), custom_call_target="tpu_custom_call" | custom-call | tf_op jit(solution)/shard_map/pallas_call | solution.py:304
  42.8 1.9 %copy.7 = f32[256,512]{1,0:T(8,128)} copy(f32[256,512]{1,0:T(8,128)} %shard_map.37) | data formatting | bytes 1048576
Async XLA Ops:
  0.7 0.7 %copy-start = (s32[1,2,1]{1,2,0:T(1,128)S(1)}, s32[1,2,1]{1,2,0:T(1,128)}, u32[]{:S(2)}) copy-start(s32[1,2,1]{1,2,0:T(1,128)} %param.5) | copy-start | bytes 28
where the time goes:
time: 44.8 us; the launch traced here: 44.6 us
  Pallas kernels  40.8 us (91%)
  local copies, waits for them, and re-layouts  3.16 us (7%)
  between operations  0.68 us (2%)
    pallas_call x1, Pallas kernels, on_device(): pl.pallas_call(functools.partial(kernel, n, ring), out_shape=jax.ShapeDty...  40.8 us
    unnamed x3, local copies, waits for them, and re-layouts  2.52 us

commit v1 on v0

--- a/solution.py
+++ b/solution.py
@@ -213,7 +213,7 @@
     scaled = (weight * inverse_of(s0[...])).astype(BF16)
     total = jnp.dot(scaled, c_ref[...], preferred_element_type=F32)
     gather_sums(ring - 1)
-    weight = amps[1, 0:1, 0:1] * amp * masks[1:2, 0:1]
+    weight = amps[1, 0:1, 0:1] * amp * masks[0:1, 1:2]
     correlation = own[...] + sum_in[0] + sum_in[1]
     scaled = (weight * inverse_of(correlation)).astype(BF16)
     total = total + jnp.dot(scaled, vis[...], preferred_element_type=F32)
@@ -301,6 +301,8 @@
     rows = size * ring // n
     width = max(rows, 128)
     dma = pltpu.SemaphoreType.DMA
+    lanes = -(-orbitals // 128) * 128
+    used = 2 * orbitals * (size * (ring + 1 + n) + width * n) + 24 * orbitals * lanes + 4 * size * (rows + width)
     return pl.pallas_call(
         functools.partial(kernel, n, ring),
         out_shape=jax.ShapeDtypeStruct((rows, size), F32),
@@ -321,9 +323,9 @@
             dma((ring, n // ring)), dma((n,)), dma((n // 2,)), dma((n,)), dma((n,)),
         ],
         compiler_params=pltpu.CompilerParams(
-            collective_id=0, has_side_effects=True, vmem_limit_bytes=60 * 1024 * 1024
+            collective_id=0, has_side_effects=True, vmem_limit_bytes=used + 4 * 1024 * 1024
         ),
-    )(block, amplitudes.reshape(1, 1), plan.reshape(2, 1))
+    )(block, amplitudes.reshape(1, 1), jnp.swapaxes(plan, 1, 2).reshape(1, 2))
 
 
 def solution(mesh):

time: 44.8 us -> 42.3 us (0.944)
  Pallas kernels: 40.8 us -> 39.1 us
  local copies, waits for them, and re-layouts: 3.16 us -> 2.37 us
    pallas_call x1, Pallas kernels: 40.8 us -> 39.1 us  [on_device(): pl.pallas_call(functools.partial(kernel, n, ring), out_shape=jax.ShapeDty...]
    reshape x1 -> x0, local copies, waits for them, and re-layouts: 0.65 us -> none  [on_device(): plan.reshape(2, 1)]
    unnamed x3 -> x5, local copies, waits for them, and re-layouts: 2.52 us -> 2.37 us
where the time goes in v1:
time: 42.3 us; the launch traced here: 42.1 us
  Pallas kernels  39.1 us (92%)
  local copies, waits for them, and re-layouts  2.37 us (6%)
  between operations  0.68 us (2%)
    pallas_call x1, Pallas kernels, on_device(): pl.pallas_call(functools.partial(kernel, n, ring), out_shape=jax.ShapeDty...  39.1 us
    unnamed x5, local copies, waits for them, and re-layouts  2.37 us

profile of v1, /device:TPU:7, one launch (start us, length us, event | category | flops | bytes accessed | tf_op | source)
XLA Modules:
  0.0 42.1 jit_solution(4388200848955273697)
XLA Ops:
  0.7 0.0 copy-start.1
  0.7 0.6 %copy-done.1 = s32[1,2,1]{1,2,0:T(1,128)S(1)} copy-done((s32[1,2,1]{1,2,0:T(1,128)S(1)}, s32[1,2,1]{1,2,0:T(1,128)}, u32[]{:S(2)}) %copy-start.1) | copy-done | bytes 32
  1.3 0.0 copy-start
  1.3 0.9 %copy-done = bf16[1,512,200]{1,2,0:T(8,128)(2,1)S(1)} copy-done((bf16[1,512,200]{1,2,0:T(8,128)(2,1)S(1)}, bf16[1,512,200]{1,2,0:T(8,128)(2,1)}, u32[]{:S(2)}) %copy-start) | copy-done | bytes 204824
  2.2 39.1 %shard_map.37 = f32[256,512]{1,0:T(8,128)S(1)} custom-call(bf16[200,512]{1,0:T(8,128)(2,1)S(1)} %bitcast.6, bf16[1,1]{1,0:T(2,128)(2,1)} %bitcast.5.amp_ref, s32[1,2]{1,0:T(1,128)S(1)} %bitcast.7), custom_call_target="tpu_custom_call" | custom-call | tf_op jit(solution)/shard_map/pallas_call | solution.py:306
  41.3 0.8 %copy.6 = f32[256,512]{1,0:T(8,128)} copy(f32[256,512]{1,0:T(8,128)S(1)} %shard_map.37) | data formatting | bytes 1048576
Async XLA Ops:
  0.7 0.7 %copy-start.1 = (s32[1,2,1]{1,2,0:T(1,128)S(1)}, s32[1,2,1]{1,2,0:T(1,128)}, u32[]{:S(2)}) copy-start(s32[1,2,1]{1,2,0:T(1,128)} %param.5) | copy-start | bytes 28
  1.3 0.9 %copy-start = (bf16[1,512,200]{1,2,0:T(8,128)(2,1)S(1)}, bf16[1,512,200]{1,2,0:T(8,128)(2,1)}, u32[]{:S(2)}) copy-start(bf16[1,512,200]{1,2,0:T(8,128)(2,1)} %param.3) | copy-start | bytes 614404

commit v2 on v1

v2 whole, which is shorter than its diff:
```python
import functools

import jax
import jax.numpy as jnp
from jax import lax
from jax.experimental import pallas as pl
from jax.experimental.pallas import tpu as pltpu
from jax.sharding import PartitionSpec as P

ORDER = 2
F32 = jnp.float32
BF16 = jnp.bfloat16


def each(count, body):
    if count <= 8:
        for i in range(count):
            body(i)
    else:
        lax.fori_loop(0, count, lambda i, c: (body(i), c)[1], 0)


def inverse_of(correlation):
    size = correlation.shape[0]
    row = lax.broadcasted_iota(jnp.int32, (size, size), 0)
    col = lax.broadcasted_iota(jnp.int32, (size, size), 1)
    identity = jnp.where(row == col, 1.0, 0.0).astype(F32)
    remainder = identity - correlation
    inverse = identity + remainder
    for level in range(ORDER - 1):
        inverse = identity + jnp.dot(
            remainder, inverse, precision=lax.Precision.HIGHEST, preferred_element_type=F32
        )
    return inverse


def gram(a, b):
    return lax.dot_general(a, b, (((0,), (0,)), ((), ())), preferred_element_type=F32)


def against(a, b):
    return lax.dot_general(a, b, (((1,), (1,)), ((), ())), preferred_element_type=F32)


def parts_of(size, count):
    step = -(-size // (8 * count)) * 8
    return [(start, min(step, size - start)) for start in range(0, size, step)]


def swapped(det, index, n):
    if n & (n - 1):
        return lax.rem(det + index, n)
    bit, other = 1, det
    while bit < n:
        flip = lax.rem(index // bit, 2) * bit if not isinstance(index, int) else index // bit % 2 * bit
        other = other + flip * (1 - 2 * lax.rem(det // bit, 2))
        bit *= 2
    return other


def kernel(
    n, ring, c_ref, amp_ref, plan_ref, out_ref,
    vis, amps, own, sum_in, sum_out, pieces, folded, wide,
    local_sem, sum_send, sum_recv, vis_send, vis_recv,
    piece_send, piece_recv, pass_send, chip_send, pair_send, folded_recv,
):
    det = lax.axis_index("det")
    row = lax.axis_index("row")
    rows = out_ref.shape[0]
    width = pieces.shape[2]
    per_block = n // ring
    chips = n // 2
    chip, core = det // 2, lax.rem(det, 2)
    partner = chip * 2 + (1 - core)
    home = det // per_block
    toward = (row < ring - 1, row > 0)
    passes = ((row < ring - 1) & (row >= home), (row > 0) & (row <= home))
    relays = passes[0] | passes[1]
    steps_away = jnp.abs(row - home)
    chunks = parts_of(own.shape[1], 4)

    def remote(src, dst, send, recv, **where):
        return pltpu.make_async_remote_copy(
            src_ref=src, dst_ref=dst, send_sem=send, recv_sem=recv,
            device_id=where, device_id_type=pl.DeviceIdType.MESH,
        )

    def columns_of(target):
        start = lax.rem(target, per_block) * rows // width * width
        return c_ref.at[:, pl.ds(pl.multiple_of(start, width), width)]

    barrier = pltpu.get_barrier_semaphore()

    def greet(i):
        peer = lax.rem(det + 1 + i, n)
        pl.semaphore_signal(barrier, inc=1, device_id={"det": peer}, device_id_type=pl.DeviceIdType.MESH)

    each(n - 1, greet)

    for side in (0, 1):

        @pl.when(toward[side])
        def _():
            peer = row + 1 - 2 * side
            pl.semaphore_signal(barrier, inc=1, device_id={"row": peer}, device_id_type=pl.DeviceIdType.MESH)

    @pl.when(row == home)
    def _():
        keep = pltpu.make_async_copy(columns_of(det), pieces.at[det], local_sem)
        keep.start()
        keep.wait()

    amps[0] = jnp.broadcast_to(amp_ref[...].astype(F32), amps.shape[1:])
    own[0] = against(c_ref[...], c_ref[...])
    pl.semaphore_wait(barrier, n - 1 + toward[0].astype(jnp.int32) + toward[1].astype(jnp.int32))

    def chunk_copy(which, k, side):
        span = pl.ds(*chunks[k])
        return remote(
            sum_out.at[which, side, span], sum_in.at[which, side, span],
            sum_send.at[which, side, k], sum_recv.at[which, side, k], row=row + 1 - 2 * side,
        )

    def sums(which, side, first):
        for k, (start, length) in enumerate(chunks):
            span = pl.ds(start, length)
            if first:
                sum_in[which, side, span] = jnp.zeros((length, own.shape[2]), F32)
            else:
                chunk_copy(which, k, side).wait_recv()

            @pl.when(toward[side])
            def _():
                if first:
                    sum_out[which, side, span] = own[which, span]
                else:
                    sum_out[which, side, span] = own[which, span] + sum_in[which, side, span]
                chunk_copy(which, k, side).start()

    def gather_sums(which, distance):
        @pl.when(row == distance)
        def _():
            sums(which, 0, distance == 0)

        @pl.when(row == ring - 1 - distance)
        def _():
            sums(which, 1, distance == 0)

    def piece(k):
        target = row * per_block + k
        return target, remote(
            columns_of(target), pieces.at[det], piece_send.at[k], piece_recv.at[det], det=target
        )

    def hand_out(k, wait=False):
        target, copy = piece(k)

        @pl.when(target != det)
        def _():
            if wait:
                copy.wait_send()
            else:
                copy.start()

    def pass_copy(source, side):
        return remote(
            pieces.at[source], pieces.at[source], pass_send.at[source, side], piece_recv.at[source],
            row=row + 1 - 2 * side,
        )

    def pass_on(index):
        source = swapped(det, index, n)

        @pl.when(relays & (index >= 0) & (index < n))
        def _():
            @pl.when((row != home) | (source != det))
            def _():
                pass_copy(source, 0).wait_recv()

            for side in (0, 1):

                @pl.when(passes[side])
                def _():
                    pass_copy(source, side).start()

    share = max(n // 4, 1)

    def slot(number):
        each(share, lambda i: pass_on((number - steps_away) * share + i))

    following = lax.rem(det + 1, n)
    visit = remote(c_ref, vis, vis_send.at[0], vis_recv.at[0], det=following)
    visit_amp = remote(amps.at[0], amps.at[1], vis_send.at[1], vis_recv.at[1], det=following)
    visit.start()
    visit_amp.start()
    gather_sums(0, 0)
    each(per_block, hand_out)
    slot(0)
    visit.wait_recv()
    own[1] = against(vis[...], c_ref[...])
    gather_sums(1, 0)
    for distance in range(1, ring - 1):
        gather_sums(0, distance)
        gather_sums(1, distance)
        slot(distance)
    visit_amp.wait_recv()
    amp = amps[0, 0:1, 0:1]
    masks = plan_ref[...].astype(F32)
    gather_sums(0, ring - 1)
    weight = amp * amp * masks[0:1, 0:1]
    scaled = (weight * inverse_of(own[0] + sum_in[0, 0] + sum_in[0, 1])).astype(BF16)
    total = jnp.dot(scaled, c_ref[...], preferred_element_type=F32)
    gather_sums(1, ring - 1)
    weight = amps[1, 0:1, 0:1] * amp * masks[0:1, 1:2]
    scaled = (weight * inverse_of(own[1] + sum_in[1, 0] + sum_in[1, 1])).astype(BF16)
    total = total + jnp.dot(scaled, vis[...], preferred_element_type=F32)
    folded[det] = total.astype(BF16)

    def to_chip(i):
        target = swapped(chip, i + 1, chips) * 2 + core
        return remote(folded.at[det], folded.at[det], chip_send.at[i], folded_recv.at[det], det=target)

    def to_pair(source):
        return remote(
            folded.at[source], folded.at[source], pair_send.at[source], folded_recv.at[source], det=partner
        )

    each(chips - 1, lambda i: to_chip(i).start())
    to_pair(det).start()
    slots = -(-n // share) + ring - 2
    for number in range(ring - 1, slots):
        slot(number)

    sink = out_ref if width == rows else wide

    def add(source, first=False):
        @pl.when(jnp.logical_not(relays))
        def _():
            pass_copy(source, 0).wait_recv()

        value = gram(pieces[source], folded[source])
        sink[...] = value if first else sink[...] + value

    def landed(source):
        to_pair(source).wait_recv()

    add(det, True)
    landed(partner)
    add(partner)

    def relay(i):
        other = swapped(chip, i + 1, chips) * 2
        landed(other + core)
        to_pair(other + core).start()
        add(other + core)

    def relayed(i):
        other = swapped(chip, i + 1, chips) * 2
        landed(other + 1 - core)
        add(other + 1 - core)

    each(chips - 1, relay)
    each(chips - 1, relayed)
    if width != rows:
        out_ref[...] = wide[pl.ds(pl.multiple_of(lax.rem(det * rows, width), rows), rows)]

    visit.wait_send()
    visit_amp.wait_send()
    for side in (0, 1):

        @pl.when(toward[side])
        def _():
            for which in (0, 1):
                for k in range(len(chunks)):
                    chunk_copy(which, k, side).wait_send()

        @pl.when(passes[side])
        def _():
            each(n, lambda source: pass_copy(source, side).wait_send())

    each(per_block, lambda k: hand_out(k, wait=True))
    each(chips - 1, lambda i: to_chip(i).wait_send())
    to_pair(det).wait_send()
    each(chips - 1, lambda i: to_pair(swapped(chip, i + 1, chips) * 2 + core).wait_send())


def on_device(coefficients, amplitudes, plan):
    n, ring = lax.axis_size("det"), lax.axis_size("row")
    if coefficients.shape[0] != 1 or plan.shape[1] != 2:
        raise ValueError("unsupported sizes")
    block = jnp.swapaxes(coefficients, 1, 2)[0]
    orbitals, size = block.shape
    rows = size * ring // n
    width = max(rows, 128)
    dma = pltpu.SemaphoreType.DMA
    lanes = -(-orbitals // 128) * 128
    used = 2 * orbitals * (size * (ring + 1 + n) + width * n) + 40 * orbitals * lanes + 4 * size * (rows + width)
    return pl.pallas_call(
        functools.partial(kernel, n, ring),
        out_shape=jax.ShapeDtypeStruct((rows, size), F32),
        in_specs=[pl.BlockSpec(memory_space=pltpu.VMEM)] * 3,
        out_specs=pl.BlockSpec(memory_space=pltpu.VMEM),
        scratch_shapes=[
            pltpu.VMEM((orbitals, size), BF16),
            pltpu.VMEM((2, 8, 128), F32),
            pltpu.VMEM((2, orbitals, orbitals), F32),
            pltpu.VMEM((2, 2, orbitals, orbitals), F32),
            pltpu.VMEM((2, 2, orbitals, orbitals), F32),
            pltpu.VMEM((n, orbitals, width), BF16),
            pltpu.VMEM((n, orbitals, size), BF16),
            pltpu.VMEM((width, size) if width != rows else (8, 128), F32),
            dma, dma((2, 2, 4)), dma((2, 2, 4)), dma((2,)), dma((2,)),
            dma((n // ring,)), dma((n,)), dma((n, 2)), dma((n // 2,)), dma((n,)), dma((n,)),
        ],
        compiler_params=pltpu.CompilerParams(
            collective_id=0, has_side_effects=True, vmem_limit_bytes=used + 4 * 1024 * 1024
        ),
    )(block, amplitudes.reshape(1, 1), jnp.swapaxes(plan, 1, 2).reshape(1, 2))


def solution(mesh):
    placed = (P("det", "row", None), P("det"), P("det", None, None))
    return jax.shard_map(
        on_device, mesh=mesh, in_specs=placed, out_specs=P("det", "row"), check_vma=False
    )
```

time: 42.3 us -> 46.6 us (1.10)
  the two profiles are of different devices: /device:TPU:7 before, /device:TPU:6 now
where the time goes in v2:
time: 46.6 us; the launch traced here: 46.4 us
  Pallas kernels  43.4 us (93%)
  local copies, waits for them, and re-layouts  2.37 us (5%)
  between operations  0.68 us (1%)
    pallas_call x1, Pallas kernels, on_device(): pl.pallas_call(functools.partial(kernel, n, ring), out_shape=jax.ShapeDty...  43.4 us
    unnamed x5, local copies, waits for them, and re-layouts  2.37 us

profile of v2, /device:TPU:6, one launch (start us, length us, event | category | flops | bytes accessed | tf_op | source)
XLA Modules:
  0.0 46.4 jit_solution(5715287663644372559)
XLA Ops:
  0.7 0.0 copy-start.1
  0.7 0.6 %copy-done.1 = s32[1,2,1]{1,2,0:T(1,128)S(1)} copy-done((s32[1,2,1]{1,2,0:T(1,128)S(1)}, s32[1,2,1]{1,2,0:T(1,128)}, u32[]{:S(2)}) %copy-start.1) | copy-done | bytes 32
  1.3 0.0 copy-start
  1.3 0.9 %copy-done = bf16[1,512,200]{1,2,0:T(8,128)(2,1)S(1)} copy-done((bf16[1,512,200]{1,2,0:T(8,128)(2,1)S(1)}, bf16[1,512,200]{1,2,0:T(8,128)(2,1)}, u32[]{:S(2)}) %copy-start) | copy-done | bytes 204824
  2.2 43.4 %shard_map.37 = f32[256,512]{1,0:T(8,128)S(1)} custom-call(bf16[200,512]{1,0:T(8,128)(2,1)S(1)} %bitcast.6, bf16[1,1]{1,0:T(2,128)(2,1)} %bitcast.5.amp_ref, s32[1,2]{1,0:T(1,128)S(1)} %bitcast.7), custom_call_target="tpu_custom_call" | custom-call | tf_op jit(solution)/shard_map/pallas_call | solution.py:298
  45.6 0.8 %copy.6 = f32[256,512]{1,0:T(8,128)} copy(f32[256,512]{1,0:T(8,128)S(1)} %shard_map.37) | data formatting | bytes 1048576
Async XLA Ops:
  0.7 0.7 %copy-start.1 = (s32[1,2,1]{1,2,0:T(1,128)S(1)}, s32[1,2,1]{1,2,0:T(1,128)}, u32[]{:S(2)}) copy-start(s32[1,2,1]{1,2,0:T(1,128)} %param.5) | copy-start | bytes 28
  1.3 0.9 %copy-start = (bf16[1,512,200]{1,2,0:T(8,128)(2,1)S(1)}, bf16[1,512,200]{1,2,0:T(8,128)(2,1)}, u32[]{:S(2)}) copy-start(bf16[1,512,200]{1,2,0:T(8,128)(2,1)} %param.3) | copy-start | bytes 614404

commit v3 on v1

v3 whole, which is shorter than its diff:
```python
import functools

import jax
import jax.numpy as jnp
from jax import lax
from jax.experimental import pallas as pl
from jax.experimental.pallas import tpu as pltpu
from jax.sharding import PartitionSpec as P

ORDER = 2
F32 = jnp.float32
BF16 = jnp.bfloat16


def each(count, body):
    if count <= 8:
        for i in range(count):
            body(i)
    else:
        lax.fori_loop(0, count, lambda i, c: (body(i), c)[1], 0)


def inverse_of(correlation):
    size = correlation.shape[0]
    row = lax.broadcasted_iota(jnp.int32, (size, size), 0)
    col = lax.broadcasted_iota(jnp.int32, (size, size), 1)
    identity = jnp.where(row == col, 1.0, 0.0).astype(F32)
    remainder = identity - correlation
    inverse = identity + remainder
    for level in range(ORDER - 1):
        inverse = identity + jnp.dot(
            remainder, inverse, precision=lax.Precision.HIGHEST, preferred_element_type=F32
        )
    return inverse


def gram(a, b):
    return lax.dot_general(a, b, (((0,), (0,)), ((), ())), preferred_element_type=F32)


def against(a, b):
    return lax.dot_general(a, b, (((1,), (1,)), ((), ())), preferred_element_type=F32)


def parts_of(size, count):
    step = -(-size // (8 * count)) * 8
    return [(start, min(step, size - start)) for start in range(0, size, step)]


def splits(n, ring, size):
    halves = 2 if (n // ring) % 2 == 0 and size % 256 == 0 else 1
    chunks = 2 * halves if size % (256 * halves) == 0 else halves
    return chunks, halves


def kernel(
    n, ring, c_ref, amp_ref, plan_ref, out_ref,
    cw, vw, vis, amps, amp_in, plan_in, own, sum_in, sum_out, s0, pieces, folded, wide,
    local_sem, cw_send, cw_recv, vw_send, vw_recv, sum_send, sum_recv, vis_send, vis_recv,
    piece_send, piece_recv, near_send, relay_send, pair_send, folded_recv,
):
    det = lax.axis_index("det")
    row = lax.axis_index("row")
    rows, size = out_ref.shape
    width = pieces.shape[2]
    per_block = n // ring
    chips = n // 2
    chip, core = det // 2, lax.rem(det, 2)
    partner = chip * 2 + (1 - core)
    even = core == 0
    toward = (row < ring - 1, row > 0)
    sum_parts = parts_of(own.shape[0], 4)
    n_chunks, n_halves = splits(n, ring, size)
    chunk, half_size = size // n_chunks, size // n_halves

    def remote(src, dst, send, recv, **where):
        return pltpu.make_async_remote_copy(
            src_ref=src, dst_ref=dst, send_sem=send, recv_sem=recv,
            device_id=where, device_id_type=pl.DeviceIdType.MESH,
        )

    stage = [
        pltpu.make_async_copy(c_ref, cw.at[row], local_sem.at[0]),
        pltpu.make_async_copy(amp_ref, amp_in, local_sem.at[1]),
        pltpu.make_async_copy(plan_ref, plan_in, local_sem.at[2]),
    ]
    for copy in stage:
        copy.start()

    barrier = pltpu.get_barrier_semaphore()

    def greet(i):
        peer = lax.rem(det + 1 + i, n)
        pl.semaphore_signal(barrier, inc=1, device_id={"det": peer}, device_id_type=pl.DeviceIdType.MESH)

    each(n - 1, greet)

    for side in (0, 1):

        @pl.when(toward[side])
        def _():
            peer = row + 1 - 2 * side
            pl.semaphore_signal(barrier, inc=1, device_id={"row": peer}, device_id_type=pl.DeviceIdType.MESH)

    for copy in stage:
        copy.wait()
    amps[0] = jnp.broadcast_to(amp_in[...].astype(F32), amps.shape[1:])
    s0[...] = against(cw[row], cw[row])
    pl.semaphore_wait(barrier, n - 1 + toward[0].astype(jnp.int32) + toward[1].astype(jnp.int32))

    def along(block, side, q):
        span = cw.at[block, :, pl.ds(q * chunk, chunk)]
        return remote(
            span, span, cw_send.at[block, side, q], cw_recv.at[block, q], row=row + 1 - 2 * side
        )

    def pass_on(block, side, q, wait=False):
        @pl.when(toward[side])
        def _():
            copy = along(block, side, q)
            if wait:
                copy.wait_send()
            else:
                copy.start()

    def sum_copy(k, side):
        span = pl.ds(*sum_parts[k])
        return remote(
            sum_out.at[side, span], sum_in.at[side, span], sum_send.at[side, k], sum_recv.at[side, k],
            row=row + 1 - 2 * side,
        )

    def sums(side, first):
        for k, (start, length) in enumerate(sum_parts):
            span = pl.ds(start, length)
            if not first:
                sum_copy(k, side).wait_recv()

            @pl.when(toward[side])
            def _():
                if first:
                    sum_out[side, span] = own[span]
                else:
                    sum_out[side, span] = own[span] + sum_in[side, span]
                sum_copy(k, side).start()

    def gather_sums(distance):
        @pl.when(even & (row == distance))
        def _():
            sums(0, distance == 0)

        @pl.when(even & (row == ring - 1 - distance))
        def _():
            sums(1, distance == 0)

    def piece(block, k):
        target = block * per_block + k
        start = pl.multiple_of(k * rows // width * width, width)
        return target, remote(
            cw.at[block, :, pl.ds(start, width)], pieces.at[det],
            piece_send.at[block, k], piece_recv.at[det], det=target,
        )

    def hand_out(block, half, wait=False):
        share = per_block // n_halves

        def one(i):
            target, copy = piece(block, half * share + i)

            @pl.when(target != det)
            def _():
                if wait:
                    copy.wait_send()
                else:
                    copy.start()

        each(share, one)

    def columns(ref, block, half):
        return ref[block, :, pl.ds(half * half_size, half_size)]

    def to_partner(block, half):
        span = pl.ds(half * half_size, half_size)
        return remote(
            cw.at[block, :, span], vw.at[block, :, span], vw_send.at[block, half], vw_recv.at[block, half],
            det=partner,
        )

    following = lax.rem(det + 1, n)
    visit = remote(cw.at[row], vis, vis_send.at[0], vis_recv.at[0], det=following)
    visit_amp = remote(amps.at[0], amps.at[1], vis_send.at[1], vis_recv.at[1], det=following)
    visit.start()
    visit_amp.start()
    for q in range(n_chunks):
        for side in (0, 1):
            pass_on(row, side, q)
    for half in range(n_halves):
        hand_out(row, half)
    visit.wait_recv()
    own[...] = against(vis[...], cw[row])
    gather_sums(0)

    def blocks_at(distance):
        for side in (0, 1):
            block = row - distance if side == 0 else row + distance
            yield side, block, (block >= 0) & (block < ring)

    def arrive(distance):
        for q in range(n_chunks):
            for side, block, there in blocks_at(distance):

                @pl.when(there)
                def _():
                    along(block, side, q).wait_recv()
                    pass_on(block, side, q)
                    if (q + 1) % (n_chunks // n_halves) == 0:
                        half = q // (n_chunks // n_halves)

                        @pl.when(even)
                        def _():
                            to_partner(block, half).start()

                        hand_out(block, half)
                        part = columns(cw, block, half)
                        s0[...] += against(part, part)

    def visited(distance):
        for half in range(n_halves):
            for side, block, there in blocks_at(distance):

                @pl.when(there & jnp.logical_not(even))
                def _():
                    to_partner(block, half).wait_recv()
                    own[...] += against(columns(vw, block, half), columns(cw, block, half))

    for distance in range(1, ring):
        arrive(distance)
        if distance < ring - 1:
            visited(distance)
            gather_sums(distance)
    visit_amp.wait_recv()
    amp = amps[0, 0:1, 0:1]
    masks = plan_in[...].astype(F32)
    weight = amp * amp * masks[0:1, 0:1]
    scaled = (weight * inverse_of(s0[...])).astype(BF16)
    total = jnp.dot(scaled, cw[row], preferred_element_type=F32)
    visited(ring - 1)
    gather_sums(ring - 1)
    weight = amps[1, 0:1, 0:1] * amp * masks[0:1, 1:2]
    for side in (0, 1):

        @pl.when(even & toward[1 - side])
        def _():
            own[...] += sum_in[side]

    scaled = (weight * inverse_of(own[...])).astype(BF16)
    total = total + jnp.dot(scaled, vis[...], preferred_element_type=F32)
    folded[det] = total.astype(BF16)

    def span_of(half):
        return pl.ds(half * half_size, half_size)

    def send_folded(source, half, target, send):
        span = folded.at[source, :, span_of(half)]
        return remote(span, span, send, folded_recv.at[source, half], det=target)

    def to_pair(source, half):
        return send_folded(source, half, partner, pair_send.at[source, half])

    def landed(source, half):
        to_pair(source, half).wait_recv()

    sink = out_ref if width == rows else wide

    def piece_here(source):
        remote(
            cw.at[0, :, pl.ds(0, width)], pieces.at[source], piece_send.at[0, 0], piece_recv.at[source],
            det=partner,
        ).wait_recv()

    def add(source, half):
        sink[:, span_of(half)] += gram(pieces[source], folded[source, :, span_of(half)])

    def add_own():
        own_start = lax.rem(det, per_block) * rows // width * width
        mine = cw[det // per_block, :, pl.ds(pl.multiple_of(own_start, width), width)]
        sink[...] = gram(mine, folded[det])
        piece_here(partner)
        for half in range(n_halves):
            landed(partner, half)
            add(partner, half)

    def arrived(source, half, then=None):
        landed(source, half)
        if then is not None:
            then()
        to_pair(source, half).start()

    def foreign(source, half):
        if half == 0:
            piece_here(source)
        add(source, half)

    halves = range(n_halves)
    if chips == 4:
        across_x = chip + 1 - 2 * lax.rem(chip, 2)
        across_y = lax.rem(chip + 2, 4)
        corner = (3 - chip) * 2
        first = jnp.where(even, across_x, across_y) * 2
        second = jnp.where(even, across_y, across_x) * 2

        def near(which, half):
            target = (first if which == 0 else second) + core
            return send_folded(det, half, target, near_send.at[which, half])

        def relay(half):
            return send_folded(first + core, half, second + core, relay_send.at[half])

        for half in halves:
            near(0, half).start()
        for half in halves:
            near(1, half).start()
        for half in halves:
            to_pair(det, half).start()
        add_own()
        for half in halves:
            arrived(first + core, half, relay(half).start)
            foreign(first + core, half)
        for half in halves:
            arrived(second + core, half)
            foreign(second + core, half)
        for other in (second, first):
            for half in halves:
                landed(other + 1 - core, half)
                foreign(other + 1 - core, half)
        for half in halves:
            arrived(corner + core, half)
            foreign(corner + core, half)
        for half in halves:
            landed(corner + 1 - core, half)
            foreign(corner + 1 - core, half)
        for half in halves:
            near(0, half).wait_send()
            near(1, half).wait_send()
            relay(half).wait_send()
            for source in (det, first + core, second + core, corner + core):
                to_pair(source, half).wait_send()
    else:

        def to_chip(i, half):
            target = lax.rem(chip + 1 + i, chips) * 2 + core
            return send_folded(det, half, target, near_send.at[i, half])

        def other(i):
            return lax.rem(chip + chips - 1 - i, chips) * 2

        def relay_all(i):
            for half in halves:
                arrived(other(i) + core, half)
                foreign(other(i) + core, half)

        def relayed(i):
            for half in halves:
                landed(other(i) + 1 - core, half)
                foreign(other(i) + 1 - core, half)

        for half in halves:
            each(chips - 1, lambda i: to_chip(i, half).start())
            to_pair(det, half).start()
        add_own()
        each(chips - 1, relay_all)
        each(chips - 1, relayed)
        for half in halves:
            each(chips - 1, lambda i: to_chip(i, half).wait_send())
            to_pair(det, half).wait_send()
            each(chips - 1, lambda i: to_pair(other(i) + core, half).wait_send())
    if width != rows:
        out_ref[...] = wide[pl.ds(pl.multiple_of(lax.rem(det * rows, width), rows), rows)]

    visit.wait_send()
    visit_amp.wait_send()
    for side in (0, 1):
        for q in range(n_chunks):
            pass_on(row, side, q, wait=True)

        @pl.when(even & toward[side])
        def _():
            for k in range(len(sum_parts)):
                sum_copy(k, side).wait_send()

    for half in halves:
        hand_out(row, half, wait=True)
    for distance in range(1, ring):
        for side, block, there in blocks_at(distance):

            @pl.when(there)
            def _():
                for q in range(n_chunks):
                    pass_on(block, side, q, wait=True)
                for half in halves:
                    hand_out(block, half, wait=True)

            @pl.when(there & even)
            def _():
                for half in halves:
                    to_partner(block, half).wait_send()


def on_device(coefficients, amplitudes, plan):
    n, ring = lax.axis_size("det"), lax.axis_size("row")
    if coefficients.shape[0] != 1 or plan.shape[1] != 2:
        raise ValueError("unsupported sizes")
    block = jnp.swapaxes(coefficients, 1, 2)[0]
    orbitals, size = block.shape
    rows = size * ring // n
    width = max(rows, 128)
    chunks, halves = splits(n, ring, size)
    dma = pltpu.SemaphoreType.DMA
    lanes = -(-orbitals // 128) * 128
    used = 2 * orbitals * (size * (2 * ring + 1 + n) + width * n) + 24 * orbitals * lanes + 4 * size * (rows + width)
    return pl.pallas_call(
        functools.partial(kernel, n, ring),
        out_shape=jax.ShapeDtypeStruct((rows, size), F32),
        in_specs=[pl.BlockSpec(memory_space=pltpu.HBM)] * 3,
        out_specs=pl.BlockSpec(memory_space=pltpu.VMEM),
        scratch_shapes=[
            pltpu.VMEM((ring, orbitals, size), BF16),
            pltpu.VMEM((ring, orbitals, size), BF16),
            pltpu.VMEM((orbitals, size), BF16),
            pltpu.VMEM((2, 8, 128), F32),
            pltpu.VMEM((1, 1), amplitudes.dtype),
            pltpu.VMEM((1, 2), plan.dtype),
            pltpu.VMEM((orbitals, orbitals), F32),
            pltpu.VMEM((2, orbitals, orbitals), F32),
            pltpu.VMEM((2, orbitals, orbitals), F32),
            pltpu.VMEM((orbitals, orbitals), F32),
            pltpu.VMEM((n, orbitals, width), BF16),
            pltpu.VMEM((n, orbitals, size), BF16),
            pltpu.VMEM((width, size) if width != rows else (8, 128), F32),
            dma((3,)), dma((ring, 2, chunks)), dma((ring, chunks)), dma((ring, halves)), dma((ring, halves)),
            dma((2, 4)), dma((2, 4)), dma((2,)), dma((2,)), dma((ring, n // ring)), dma((n,)),
            dma((n // 2, halves)), dma((halves,)), dma((n, halves)), dma((n, halves)),
        ],
        compiler_params=pltpu.CompilerParams(
            collective_id=0, has_side_effects=True, vmem_limit_bytes=used + 4 * 1024 * 1024
        ),
    )(block, amplitudes.reshape(1, 1), jnp.swapaxes(plan, 1, 2).reshape(1, 2))


def solution(mesh):
    placed = (P("det", "row", None), P("det"), P("det", None, None))
    return jax.shard_map(
        on_device, mesh=mesh, in_specs=placed, out_specs=P("det", "row"), check_vma=False
    )
```

time: 42.3 us -> 38.9 us (0.920)
  the two profiles are of different devices: /device:TPU:7 before, /device:TPU:5 now
where the time goes in v3:
time: 38.9 us; the launch traced here: 38.7 us
  Pallas kernels  35.7 us (92%)
  local copies, waits for them, and re-layouts  2.37 us (6%)
  between operations  0.68 us (2%)
    pallas_call x1, Pallas kernels, on_device(): pl.pallas_call(functools.partial(kernel, n, ring), out_shape=jax.ShapeDty...  35.7 us
    unnamed x5, local copies, waits for them, and re-layouts  2.37 us

profile of v3, /device:TPU:5, one launch (start us, length us, event | category | flops | bytes accessed | tf_op | source)
XLA Modules:
  0.0 38.7 jit_solution(3570055600909652154)
XLA Ops:
  0.7 0.0 copy-start.1
  0.7 0.6 %copy-done.1 = s32[1,2,1]{1,2,0:T(1,128)S(1)} copy-done((s32[1,2,1]{1,2,0:T(1,128)S(1)}, s32[1,2,1]{1,2,0:T(1,128)}, u32[]{:S(2)}) %copy-start.1) | copy-done | bytes 32
  1.3 0.0 copy-start
  1.3 0.9 %copy-done = bf16[1,512,200]{1,2,0:T(8,128)(2,1)S(1)} copy-done((bf16[1,512,200]{1,2,0:T(8,128)(2,1)S(1)}, bf16[1,512,200]{1,2,0:T(8,128)(2,1)}, u32[]{:S(2)}) %copy-start) | copy-done | bytes 204824
  2.2 35.7 %shard_map.37 = f32[256,512]{1,0:T(8,128)S(1)} custom-call(bf16[200,512]{1,0:T(8,128)(2,1)S(1)} %bitcast.6, bf16[1,1]{1,0:T(2,128)(2,1)} %bitcast.5.amp_ref, s32[1,2]{1,0:T(1,128)S(1)} %bitcast.7), custom_call_target="tpu_custom_call" | custom-call | tf_op jit(solution)/shard_map/pallas_call | solution.py:421
  37.9 0.8 %copy.6 = f32[256,512]{1,0:T(8,128)} copy(f32[256,512]{1,0:T(8,128)S(1)} %shard_map.37) | data formatting | bytes 1048576
Async XLA Ops:
  0.7 0.7 %copy-start.1 = (s32[1,2,1]{1,2,0:T(1,128)S(1)}, s32[1,2,1]{1,2,0:T(1,128)}, u32[]{:S(2)}) copy-start(s32[1,2,1]{1,2,0:T(1,128)} %param.5) | copy-start | bytes 28
  1.3 0.9 %copy-start = (bf16[1,512,200]{1,2,0:T(8,128)(2,1)S(1)}, bf16[1,512,200]{1,2,0:T(8,128)(2,1)}, u32[]{:S(2)}) copy-start(bf16[1,512,200]{1,2,0:T(8,128)(2,1)} %param.3) | copy-start | bytes 614404

commit v4 on v3

--- a/solution.py
+++ b/solution.py
@@ -444,7 +444,11 @@
         compiler_params=pltpu.CompilerParams(
             collective_id=0, has_side_effects=True, vmem_limit_bytes=used + 4 * 1024 * 1024
         ),
-    )(block, amplitudes.reshape(1, 1), jnp.swapaxes(plan, 1, 2).reshape(1, 2))
+    )(
+        pltpu.with_memory_space_constraint(block, pltpu.HBM),
+        amplitudes.reshape(1, 1),
+        pltpu.with_memory_space_constraint(jnp.swapaxes(plan, 1, 2).reshape(1, 2), pltpu.HBM),
+    )
 
 
 def solution(mesh):

time: 38.9 us -> 37.1 us (0.954)
  local copies, waits for them, and re-layouts: 2.37 us -> 0.8 us
    unnamed x5 -> x1, local copies, waits for them, and re-layouts: 2.37 us -> 0.8 us
where the time goes in v4:
time: 37.1 us; the launch traced here: 36.9 us
  Pallas kernels  35.5 us (96%)
  local copies, waits for them, and re-layouts  0.8 us (2%)
  between operations  0.67 us (2%)
    pallas_call x1, Pallas kernels, on_device(): pl.pallas_call(functools.partial(kernel, n, ring), out_shape=jax.ShapeDty...  35.5 us
    unnamed x1, local copies, waits for them, and re-layouts  0.8 us

profile of v4, /device:TPU:5, one launch (start us, length us, event | category | flops | bytes accessed | tf_op | source)
XLA Modules:
  0.0 36.9 jit_solution(14998739645899304998)
XLA Ops:
  0.7 35.5 %shard_map.37 = f32[256,512]{1,0:T(8,128)S(1)} custom-call(bf16[200,512]{1,0:T(8,128)(2,1)} %bitcast.6, bf16[1,1]{1,0:T(2,128)(2,1)} %bitcast.5.amp_ref, s32[1,2]{1,0:T(1,128)} %bitcast.7), custom_call_target="tpu_custom_call" | custom-call | tf_op jit(solution)/shard_map/pallas_call | solution.py:421
  36.1 0.8 %copy.6 = f32[256,512]{1,0:T(8,128)} copy(f32[256,512]{1,0:T(8,128)S(1)} %shard_map.37) | data formatting | bytes 1048576

commit v5 on v4

--- a/solution.py
+++ b/solution.py
@@ -55,9 +55,9 @@
 
 def kernel(
     n, ring, c_ref, amp_ref, plan_ref, out_ref,
-    cw, vw, vis, amps, amp_in, plan_in, own, sum_in, sum_out, s0, pieces, folded, wide,
+    cw, vw, vis, scaled, amps, amp_in, plan_in, own, sum_in, sum_out, s0, pieces, folded, wide,
     local_sem, cw_send, cw_recv, vw_send, vw_recv, sum_send, sum_recv, vis_send, vis_recv,
-    piece_send, piece_recv, near_send, relay_send, pair_send, folded_recv,
+    piece_send, piece_recv, throw_send, serve_send, serve_recv, near_send, relay_send, pair_send, folded_recv,
 ):
     det = lax.axis_index("det")
     row = lax.axis_index("row")
@@ -68,6 +68,13 @@
     chip, core = det // 2, lax.rem(det, 2)
     partner = chip * 2 + (1 - core)
     even = core == 0
+    quad = chips == 4 and per_block == 2
+    home, corner = det // per_block, chips - 1 - chip
+    served = ring >= 4
+    reach = ring - 2 if served else ring - 1
+    at_end = (row == 0) | (row == ring - 1)
+    serves = even & ((row == 1) | (row == ring - 2))
+    throws = (row == home) & ((row == 0) | (row == ring - 1))
     toward = (row < ring - 1, row > 0)
     sum_parts = parts_of(own.shape[0], 4)
     n_chunks, n_halves = splits(n, ring, size)
@@ -130,28 +137,26 @@
             row=row + 1 - 2 * side,
         )
 
-    def sums(side, first):
+    def sums(side, distance):
         for k, (start, length) in enumerate(sum_parts):
             span = pl.ds(start, length)
-            if not first:
+            if distance:
                 sum_copy(k, side).wait_recv()
-
-            @pl.when(toward[side])
-            def _():
-                if first:
-                    sum_out[side, span] = own[span]
-                else:
-                    sum_out[side, span] = own[span] + sum_in[side, span]
+            if distance < reach:
+                sum_out[side, span] = own[span] + sum_in[side, span] if distance else own[span]
                 sum_copy(k, side).start()
 
     def gather_sums(distance):
+        if distance > reach:
+            return
+
         @pl.when(even & (row == distance))
         def _():
-            sums(0, distance == 0)
+            sums(0, distance)
 
         @pl.when(even & (row == ring - 1 - distance))
         def _():
-            sums(1, distance == 0)
+            sums(1, distance)
 
     def piece(block, k):
         target = block * per_block + k
@@ -167,7 +172,11 @@
         def one(i):
             target, copy = piece(block, half * share + i)
 
-            @pl.when(target != det)
+            direct = target != det
+            if quad:
+                direct &= (jnp.abs(block - row) < ring - 1) | (corner != block)
+
+            @pl.when(direct)
             def _():
                 if wait:
                     copy.wait_send()
@@ -175,6 +184,21 @@
                     copy.start()
 
         each(share, one)
+
+    def thrown(i, wait=False):
+        source = corner * 2 + i
+        copy = remote(
+            pieces.at[source], pieces.at[source], throw_send.at[i], piece_recv.at[source],
+            row=ring - 1 - row,
+        )
+
+        @pl.when(throws)
+        def _():
+            if wait:
+                copy.wait_send()
+            else:
+                copy.wait_recv()
+                copy.start()
 
     def columns(ref, block, half):
         return ref[block, :, pl.ds(half * half_size, half_size)]
@@ -194,11 +218,11 @@
     for q in range(n_chunks):
         for side in (0, 1):
             pass_on(row, side, q)
-    for half in range(n_halves):
-        hand_out(row, half)
     visit.wait_recv()
     own[...] = against(vis[...], cw[row])
     gather_sums(0)
+    for half in range(n_halves):
+        hand_out(row, half)
 
     def blocks_at(distance):
         for side in (0, 1):
@@ -241,20 +265,35 @@
     visit_amp.wait_recv()
     amp = amps[0, 0:1, 0:1]
     masks = plan_in[...].astype(F32)
+    is_served = even & at_end if served else jnp.bool_(False)
+    serve = remote(scaled.at[1], scaled.at[1], serve_send, serve_recv, row=jnp.where(row == 1, 0, ring - 1))
+
+    def scale_visitor():
+        for side in (0, 1):
+
+            @pl.when(even & toward[1 - side])
+            def _():
+                own[...] += sum_in[side]
+
+        weight = amps[1, 0:1, 0:1] * amp * masks[0:1, 1:2]
+        scaled[1] = (weight * inverse_of(own[...])).astype(BF16)
+
+    if served:
+
+        @pl.when(serves)
+        def _():
+            scale_visitor()
+            serve.start()
+
     weight = amp * amp * masks[0:1, 0:1]
-    scaled = (weight * inverse_of(s0[...])).astype(BF16)
-    total = jnp.dot(scaled, cw[row], preferred_element_type=F32)
+    scaled[0] = (weight * inverse_of(s0[...])).astype(BF16)
+    total = jnp.dot(scaled[0], cw[row], preferred_element_type=F32)
     visited(ring - 1)
     gather_sums(ring - 1)
-    weight = amps[1, 0:1, 0:1] * amp * masks[0:1, 1:2]
-    for side in (0, 1):
-
-        @pl.when(even & toward[1 - side])
-        def _():
-            own[...] += sum_in[side]
-
-    scaled = (weight * inverse_of(own[...])).astype(BF16)
-    total = total + jnp.dot(scaled, vis[...], preferred_element_type=F32)
+    pl.when(jnp.logical_not(is_served | serves) if served else jnp.bool_(True))(scale_visitor)
+    if served:
+        pl.when(is_served)(serve.wait_recv)
+    total = total + jnp.dot(scaled[1], vis[...], preferred_element_type=F32)
     folded[det] = total.astype(BF16)
 
     def span_of(half):
@@ -296,16 +335,20 @@
             then()
         to_pair(source, half).start()
 
-    def foreign(source, half):
+    def foreign(source, half, detoured=False):
         if half == 0:
-            piece_here(source)
+
+            @pl.when(jnp.logical_not(detoured & throws))
+            def _():
+                piece_here(source)
+
         add(source, half)
 
     halves = range(n_halves)
-    if chips == 4:
+    if quad:
         across_x = chip + 1 - 2 * lax.rem(chip, 2)
         across_y = lax.rem(chip + 2, 4)
-        corner = (3 - chip) * 2
+        far = corner * 2
         first = jnp.where(even, across_x, across_y) * 2
         second = jnp.where(even, across_y, across_x) * 2
 
@@ -316,35 +359,44 @@
         def relay(half):
             return send_folded(first + core, half, second + core, relay_send.at[half])
 
+        def across(half):
+            return send_folded(det, half, far + core, relay_send.at[half])
+
         for half in halves:
             near(0, half).start()
-        for half in halves:
-            near(1, half).start()
         for half in halves:
             to_pair(det, half).start()
         add_own()
         for half in halves:
+            near(1, half).start()
+        thrown(0)
+        thrown(1)
+        for half in halves:
             arrived(first + core, half, relay(half).start)
+        for half in halves:
             foreign(first + core, half)
         for half in halves:
             arrived(second + core, half)
+        for half in halves:
             foreign(second + core, half)
         for other in (second, first):
             for half in halves:
                 landed(other + 1 - core, half)
                 foreign(other + 1 - core, half)
         for half in halves:
-            arrived(corner + core, half)
-            foreign(corner + core, half)
-        for half in halves:
-            landed(corner + 1 - core, half)
-            foreign(corner + 1 - core, half)
+            arrived(far + core, half)
+            foreign(far + core, half, True)
+        for half in halves:
+            landed(far + 1 - core, half)
+            foreign(far + 1 - core, half, True)
         for half in halves:
             near(0, half).wait_send()
             near(1, half).wait_send()
             relay(half).wait_send()
-            for source in (det, first + core, second + core, corner + core):
+            for source in (det, first + core, second + core, far + core):
                 to_pair(source, half).wait_send()
+        thrown(0, wait=True)
+        thrown(1, wait=True)
     else:
 
         def to_chip(i, half):
@@ -377,13 +429,17 @@
     if width != rows:
         out_ref[...] = wide[pl.ds(pl.multiple_of(lax.rem(det * rows, width), rows), rows)]
 
+    if served:
+        pl.when(serves)(serve.wait_send)
     visit.wait_send()
     visit_amp.wait_send()
     for side in (0, 1):
         for q in range(n_chunks):
             pass_on(row, side, q, wait=True)
 
-        @pl.when(even & toward[side])
+        passed = row < reach if side == 0 else row > ring - 1 - reach
+
+        @pl.when(even & passed)
         def _():
             for k in range(len(sum_parts)):
                 sum_copy(k, side).wait_send()
@@ -417,7 +473,7 @@
     chunks, halves = splits(n, ring, size)
     dma = pltpu.SemaphoreType.DMA
     lanes = -(-orbitals // 128) * 128
-    used = 2 * orbitals * (size * (2 * ring + 1 + n) + width * n) + 24 * orbitals * lanes + 4 * size * (rows + width)
+    used = 2 * orbitals * (size * (2 * ring + 1 + n) + width * n) + 28 * orbitals * lanes + 4 * size * (rows + width)
     return pl.pallas_call(
         functools.partial(kernel, n, ring),
         out_shape=jax.ShapeDtypeStruct((rows, size), F32),
@@ -427,6 +483,7 @@
             pltpu.VMEM((ring, orbitals, size), BF16),
             pltpu.VMEM((ring, orbitals, size), BF16),
             pltpu.VMEM((orbitals, size), BF16),
+            pltpu.VMEM((2, orbitals, orbitals), BF16),
             pltpu.VMEM((2, 8, 128), F32),
             pltpu.VMEM((1, 1), amplitudes.dtype),
             pltpu.VMEM((1, 2), plan.dtype),
@@ -438,7 +495,7 @@
             pltpu.VMEM((n, orbitals, size), BF16),
             pltpu.VMEM((width, size) if width != rows else (8, 128), F32),
             dma((3,)), dma((ring, 2, chunks)), dma((ring, chunks)), dma((ring, halves)), dma((ring, halves)),
-            dma((2, 4)), dma((2, 4)), dma((2,)), dma((2,)), dma((ring, n // ring)), dma((n,)),
+            dma((2, 4)), dma((2, 4)), dma((2,)), dma((2,)), dma((ring, n // ring)), dma((n,)), dma((2,)), dma, dma,
             dma((n // 2, halves)), dma((halves,)), dma((n, halves)), dma((n, halves)),
         ],
         compiler_params=pltpu.CompilerParams(

time: 37.1 us -> 35.9 us (0.968)
  the two profiles are of different devices: /device:TPU:5 before, /device:TPU:1 now
where the time goes in v5:
time: 35.9 us; the launch traced here: 35.8 us
  Pallas kernels  34.3 us (96%)
  local copies, waits for them, and re-layouts  0.8 us (2%)
  between operations  0.67 us (2%)
    pallas_call x1, Pallas kernels, on_device(): pl.pallas_call(functools.partial(kernel, n, ring), out_shape=jax.ShapeDty...  34.3 us
    unnamed x1, local copies, waits for them, and re-layouts  0.8 us

profile of v5, /device:TPU:1, one launch (start us, length us, event | category | flops | bytes accessed | tf_op | source)
XLA Modules:
  0.0 35.8 jit_solution(6965112142042020914)
XLA Ops:
  0.7 34.3 %shard_map.37 = f32[256,512]{1,0:T(8,128)S(1)} custom-call(bf16[200,512]{1,0:T(8,128)(2,1)} %bitcast.6, bf16[1,1]{1,0:T(2,128)(2,1)} %bitcast.5.amp_ref, s32[1,2]{1,0:T(1,128)} %bitcast.7), custom_call_target="tpu_custom_call" | custom-call | tf_op jit(solution)/shard_map/pallas_call | solution.py:477
  35.0 0.8 %copy.6 = f32[256,512]{1,0:T(8,128)} copy(f32[256,512]{1,0:T(8,128)S(1)} %shard_map.37) | data formatting | bytes 1048576

commit v6 on v5

--- a/solution.py
+++ b/solution.py
@@ -383,12 +383,19 @@
             for half in halves:
                 landed(other + 1 - core, half)
                 foreign(other + 1 - core, half)
+        for i in (0, 1):
+
+            @pl.when(jnp.logical_not(throws))
+            def _():
+                piece_here(far + i)
+
         for half in halves:
             arrived(far + core, half)
-            foreign(far + core, half, True)
+        both = pieces[pl.ds(far, 2)].reshape(-1, width)
         for half in halves:
             landed(far + 1 - core, half)
-            foreign(far + 1 - core, half, True)
+            part = folded[pl.ds(far, 2), :, span_of(half)].reshape(-1, half_size)
+            sink[:, span_of(half)] += gram(both, part)
         for half in halves:
             near(0, half).wait_send()
             near(1, half).wait_send()

time: 35.9 us -> 36 us (level)
  no operation moved by 1% of the time
where the time goes in v6:
time: 36 us; the launch traced here: 35.8 us
  Pallas kernels  34.4 us (96%)
  local copies, waits for them, and re-layouts  0.8 us (2%)
  between operations  0.67 us (2%)
    pallas_call x1, Pallas kernels, on_device(): pl.pallas_call(functools.partial(kernel, n, ring), out_shape=jax.ShapeDty...  34.4 us
    unnamed x1, local copies, waits for them, and re-layouts  0.8 us

profile of v6, /device:TPU:1, one launch (start us, length us, event | category | flops | bytes accessed | tf_op | source)
XLA Modules:
  0.0 35.8 jit_solution(10603107986540999887)
XLA Ops:
  0.7 34.4 %shard_map.37 = f32[256,512]{1,0:T(8,128)S(1)} custom-call(bf16[200,512]{1,0:T(8,128)(2,1)} %bitcast.6, bf16[1,1]{1,0:T(2,128)(2,1)} %bitcast.5.amp_ref, s32[1,2]{1,0:T(1,128)} %bitcast.7), custom_call_target="tpu_custom_call" | custom-call | tf_op jit(solution)/shard_map/pallas_call | solution.py:484
  35.0 0.8 %copy.6 = f32[256,512]{1,0:T(8,128)} copy(f32[256,512]{1,0:T(8,128)S(1)} %shard_map.37) | data formatting | bytes 1048576

commit v7 on v5

--- a/solution.py
+++ b/solution.py
@@ -293,8 +293,11 @@
     pl.when(jnp.logical_not(is_served | serves) if served else jnp.bool_(True))(scale_visitor)
     if served:
         pl.when(is_served)(serve.wait_recv)
-    total = total + jnp.dot(scaled[1], vis[...], preferred_element_type=F32)
-    folded[det] = total.astype(BF16)
+
+    def fold(half):
+        start = half * half_size
+        part = jnp.dot(scaled[1], vis[:, start : start + half_size], preferred_element_type=F32)
+        folded[det, :, span_of(half)] = (total[:, start : start + half_size] + part).astype(BF16)
 
     def span_of(half):
         return pl.ds(half * half_size, half_size)
@@ -363,6 +366,7 @@
             return send_folded(det, half, far + core, relay_send.at[half])
 
         for half in halves:
+            fold(half)
             near(0, half).start()
         for half in halves:
             to_pair(det, half).start()
@@ -417,6 +421,7 @@
                 foreign(other(i) + 1 - core, half)
 
         for half in halves:
+            fold(half)
             each(chips - 1, lambda i: to_chip(i, half).start())
             to_pair(det, half).start()
         add_own()

time: 35.9 us -> 35.7 us (level)
  no operation moved by 1% of the time
where the time goes in v7:
time: 35.7 us; the launch traced here: 35.5 us
  Pallas kernels  34 us (95%)
  local copies, waits for them, and re-layouts  0.8 us (2%)
  between operations  0.67 us (2%)
    pallas_call x1, Pallas kernels, on_device(): pl.pallas_call(functools.partial(kernel, n, ring), out_shape=jax.ShapeDty...  34 us
    unnamed x1, local copies, waits for them, and re-layouts  0.8 us

profile of v7, /device:TPU:1, one launch (start us, length us, event | category | flops | bytes accessed | tf_op | source)
XLA Modules:
  0.0 35.5 jit_solution(5865941802407019950)
XLA Ops:
  0.7 34.0 %shard_map.37 = f32[256,512]{1,0:T(8,128)S(1)} custom-call(bf16[200,512]{1,0:T(8,128)(2,1)} %bitcast.6, bf16[1,1]{1,0:T(2,128)(2,1)} %bitcast.5.amp_ref, s32[1,2]{1,0:T(1,128)} %bitcast.7), custom_call_target="tpu_custom_call" | custom-call | tf_op jit(solution)/shard_map/pallas_call | solution.py:482
  34.7 0.8 %copy.6 = f32[256,512]{1,0:T(8,128)} copy(f32[256,512]{1,0:T(8,128)S(1)} %shard_map.37) | data formatting | bytes 1048576

commit v8 on v5

--- a/solution.py
+++ b/solution.py
@@ -86,6 +86,21 @@
             device_id=where, device_id_type=pl.DeviceIdType.MESH,
         )
 
+    barrier = pltpu.get_barrier_semaphore()
+
+    def greet(i):
+        peer = lax.rem(det + 1 + i, n)
+        pl.semaphore_signal(barrier, inc=1, device_id={"det": peer}, device_id_type=pl.DeviceIdType.MESH)
+
+    each(n - 1, greet)
+
+    for side in (0, 1):
+
+        @pl.when(toward[side])
+        def _():
+            peer = row + 1 - 2 * side
+            pl.semaphore_signal(barrier, inc=1, device_id={"row": peer}, device_id_type=pl.DeviceIdType.MESH)
+
     stage = [
         pltpu.make_async_copy(c_ref, cw.at[row], local_sem.at[0]),
         pltpu.make_async_copy(amp_ref, amp_in, local_sem.at[1]),
@@ -93,21 +108,6 @@
     ]
     for copy in stage:
         copy.start()
-
-    barrier = pltpu.get_barrier_semaphore()
-
-    def greet(i):
-        peer = lax.rem(det + 1 + i, n)
-        pl.semaphore_signal(barrier, inc=1, device_id={"det": peer}, device_id_type=pl.DeviceIdType.MESH)
-
-    each(n - 1, greet)
-
-    for side in (0, 1):
-
-        @pl.when(toward[side])
-        def _():
-            peer = row + 1 - 2 * side
-            pl.semaphore_signal(barrier, inc=1, device_id={"row": peer}, device_id_type=pl.DeviceIdType.MESH)
 
     for copy in stage:
         copy.wait()

time: 35.9 us -> 35.9 us (level)
  no operation moved by 1% of the time
where the time goes in v8:
time: 35.9 us; the launch traced here: 35.8 us
  Pallas kernels  34.3 us (96%)
  local copies, waits for them, and re-layouts  0.8 us (2%)
  between operations  0.67 us (2%)
    pallas_call x1, Pallas kernels, on_device(): pl.pallas_call(functools.partial(kernel, n, ring), out_shape=jax.ShapeDty...  34.3 us
    unnamed x1, local copies, waits for them, and re-layouts  0.8 us

profile of v8, /device:TPU:1, one launch (start us, length us, event | category | flops | bytes accessed | tf_op | source)
XLA Modules:
  0.0 35.8 jit_solution(13882176436205873021)
XLA Ops:
  0.7 34.3 %shard_map.37 = f32[256,512]{1,0:T(8,128)S(1)} custom-call(bf16[200,512]{1,0:T(8,128)(2,1)} %bitcast.6, bf16[1,1]{1,0:T(2,128)(2,1)} %bitcast.5.amp_ref, s32[1,2]{1,0:T(1,128)} %bitcast.7), custom_call_target="tpu_custom_call" | custom-call | tf_op jit(solution)/shard_map/pallas_call | solution.py:477
  35.0 0.8 %copy.6 = f32[256,512]{1,0:T(8,128)} copy(f32[256,512]{1,0:T(8,128)S(1)} %shard_map.37) | data formatting | bytes 1048576
